TPU v7x, 256 devices: a whole 4x4x8 slice. The times are simulated.
256 devices in a mesh: head: 8 (over x, core), seq: 32 (over z, y).
Axes of the slice: x: 4, y: 4, z: 8, core: 2. Of those that a mesh axis runs over, the one named last changes fastest.
Arguments:
- queries: bfloat16 [16384, 128, 128], P(('seq', 'head')), may hold values from -12 to 12
- keys: bfloat16 [16384, 8, 128], P(('seq', 'head')), may hold values from -7.5 to 7.5
- values: bfloat16 [16384, 8, 128], P(('seq', 'head')), may hold values from -6 to 6
- doc_ids: int32 [16384], replicated, may hold values from 0 to 31, never falling along the last dimension, each value on 1 to 2048 neighbouring positions
Outputs:
- attn_out: bfloat16 [16384, 128, 128], P('seq', 'head')
Inputs may be any that keep to these rules, and one draw needn't show every extreme that they name: `doc_ids`: document numbers never fall along the sequence; every document holds 1 to 2048 tokens and one holds exactly 2048.
All inputs are finite; a program needn't handle non-finite values.
Results may differ from a plain program's by a relative error of at most 0.0031.
Values may be sent and summed in bfloat16 or wider, within the bound.
A program may use at most 64 MiB of HBM per device.

v0:
```python
import math

import jax
import jax.numpy as jnp
from jax import lax
from jax.sharding import PartitionSpec as P

REACH = 4


def from_behind(block, axis, distance):
    devices = range(lax.axis_size(axis))
    route = [(i - distance, i) for i in devices if i - distance in devices]
    return lax.ppermute(block, axis, route)


def update_carried(carried, grouped_q, key_tile, value_tile, allowed):
    run_max, run_sum, run_acc = carried
    score_scale = 1.0 / math.sqrt(grouped_q.shape[-1])
    scores = (
        jnp.einsum("tghd,sgd->tghs", grouped_q, key_tile, preferred_element_type=jnp.float32)
        * score_scale
    )
    allowed_b = allowed[:, None, None, :]
    masked = jnp.where(allowed_b, scores, -1e30)
    new_max = jnp.maximum(run_max, jnp.max(masked, axis=-1))
    weights = jnp.where(allowed_b, jnp.exp(masked - new_max[..., None]), 0.0)
    factor = jnp.exp(run_max - new_max)
    new_sum = run_sum * factor + jnp.sum(weights, axis=-1)
    new_acc = run_acc * factor[..., None] + jnp.einsum(
        "tghs,sgd->tghd",
        weights.astype(jnp.bfloat16),
        value_tile,
        preferred_element_type=jnp.float32,
    )
    return (new_max, new_sum, new_acc)


def span_needed(q_pos, q_doc, k_pos, k_doc):
    return (k_doc[-1] >= q_doc[0]) & (k_doc[0] <= q_doc[-1]) & (k_pos[0] <= q_pos[-1])


def keep_carried(carry_in):
    return carry_in


def attend_span(carried, grouped_q, q_pos, q_doc, key_block, value_block, k_pos, k_doc):
    allowed = (q_doc[:, None] == k_doc[None, :]) & (k_pos[None, :] <= q_pos[:, None])
    needed = span_needed(q_pos, q_doc, k_pos, k_doc)

    def run_block(carry_in):
        carry_in = update_carried(carry_in, grouped_q, key_block, value_block, allowed)
        return carry_in

    carried = lax.cond(needed, run_block, keep_carried, carried)
    return carried


def per_device(queries, keys, values, doc_ids):
    seq_index = lax.axis_index("seq")
    head_width = queries.shape[-1]
    local_q, local_k, local_v = (
        lax.all_to_all(queries, "head", split_axis=1, concat_axis=0, tiled=True),
        lax.all_to_all(keys, "head", split_axis=1, concat_axis=0, tiled=True),
        lax.all_to_all(values, "head", split_axis=1, concat_axis=0, tiled=True),
    )
    key_count = local_k.shape[0]
    q_start = seq_index * key_count
    q_rows = local_q.shape[0]
    kv_groups = local_k.shape[1]
    grouped_q = local_q.reshape(q_rows, kv_groups, local_q.shape[1] // kv_groups, head_width)
    q_pos = q_start + jnp.arange(q_rows, dtype=jnp.int32)
    q_doc = lax.dynamic_slice_in_dim(doc_ids, q_start, q_rows)
    carried = (
        jnp.full(grouped_q.shape[:3], -1e30, jnp.float32),
        jnp.zeros(grouped_q.shape[:3], jnp.float32),
        jnp.zeros(grouped_q.shape, jnp.float32),
    )
    offsets = jnp.arange(key_count, dtype=jnp.int32)
    own_start = seq_index * key_count
    own_doc = lax.dynamic_slice_in_dim(doc_ids, own_start, key_count)
    carried = attend_span(
        carried, grouped_q, q_pos, q_doc, local_k, local_v, own_start + offsets, own_doc
    )
    stacked = jnp.stack((local_k, local_v))
    moving = stacked
    for distance in range(1, REACH + 1):
        moving = from_behind(moving, "seq", 1)
        source = seq_index - distance
        src_start = source * key_count
        src_doc = lax.dynamic_slice_in_dim(doc_ids, jnp.maximum(src_start, 0), key_count)
        k_doc = jnp.where(source >= 0, src_doc, -1)
        carried = attend_span(
            carried, grouped_q, q_pos, q_doc, moving[0], moving[1], src_start + offsets, k_doc
        )
    run_max, run_sum, run_acc = carried
    result = (run_acc / run_sum[..., None]).astype(jnp.bfloat16).reshape(q_rows, -1, head_width)
    return result


def solution(mesh):
    in_specs = (
        P(("seq", "head"), None, None),
        P(("seq", "head"), None, None),
        P(("seq", "head"), None, None),
        P(),
    )
    out_specs = P("seq", "head", None)
    return jax.shard_map(
        per_device, mesh=mesh, in_specs=in_specs, out_specs=out_specs, check_vma=False
    )
```

profile of v0, /device:TPU:136, one launch (start us, length us, event | category | flops | bytes accessed | tf_op | source)
XLA Modules:
  0.0 167.6 jit_solution(5208430024508983708)
XLA Ops:
  0.0 1.6 copy.22
  1.6 4.3 %all-to-all-start = ((bf16[64,8,128]{2,0,1:T(8,128)(2,1)}), bf16[64,8,128]{2,0,1:T(8,128)(2,1)S(1)}, u32[]{:S(2)}, u32[]{:S(2)}) async-start(bf16[64,8,128]{2,0,1:T(8,128)(2,1)} %copy.22), calls=%async_computation | async-start | bytes 262144 | tf_op jit(solution)/shard_map/all_to_all | solution.py:64
  5.9 1.6 copy.25
  7.5 4.5 %all-to-all-done = bf16[64,8,128]{2,0,1:T(8,128)(2,1)S(1)} async-done(((bf16[64,8,128]{2,0,1:T(8,128)(2,1)}), bf16[64,8,128]{2,0,1:T(8,128)(2,1)S(1)}, u32[]{:S(2)}, u32[]{:S(2)}) %all-to-all-start) | async-done | bytes 131104 | tf_op jit(solution)/shard_map/all_to_all | solution.py:64
  12.0 3.4 %all-to-all-start.2 = ((bf16[64,8,128]{2,0,1:T(8,128)(2,1)}), bf16[64,8,128]{2,0,1:T(8,128)(2,1)S(1)}, u32[]{:S(2)}, u32[]{:S(2)}) async-start(bf16[64,8,128]{2,0,1:T(8,128)(2,1)} %copy.25), calls=%async_computation.2 | async-start | bytes 262144 | tf_op jit(solution)/shard_map/all_to_all | solution.py:65
  15.4 4.3 %copy.23 = bf16[64,128,128]{2,0,1:T(8,128)(2,1)} copy(bf16[64,128,128]{2,1,0:T(8,128)(2,1)} %param.14) | data formatting | bytes 4194304 | tf_op args[0]
  19.7 1.7 %all-to-all-done.2 = bf16[64,8,128]{2,0,1:T(8,128)(2,1)S(1)} async-done(((bf16[64,8,128]{2,0,1:T(8,128)(2,1)}), bf16[64,8,128]{2,0,1:T(8,128)(2,1)S(1)}, u32[]{:S(2)}, u32[]{:S(2)}) %all-to-all-start.2) | async-done | bytes 131104 | tf_op jit(solution)/shard_map/all_to_all | solution.py:65
  21.4 3.6 %all-to-all-start.1 = ((bf16[64,128,128]{2,0,1:T(8,128)(2,1)}), bf16[64,128,128]{2,0,1:T(8,128)(2,1)S(1)}, u32[]{:S(2)}, u32[]{:S(2)}) async-start(bf16[64,128,128]{2,0,1:T(8,128)(2,1)} %copy.23), calls=%async_computation.1 | async-start | bytes 4194304 | tf_op jit(solution)/shard_map/all_to_all | solution.py:63
  25.0 0.9 dynamic-slice_select_fusion
  26.0 0.6 fusion.98
  26.6 3.5 %collective-permute-start = (bf16[2,512,1,128]{3,1,2,0:T(8,128)(2,1)S(1)}, bf16[2,512,1,128]{3,1,2,0:T(8,128)(2,1)S(1)}, u32[]{:S(2)}, u32[]{:S(2)}) collective-permute-start(bf16[2,512,1,128]{3,1,2,0:T(8,128)(2,1)S(1)} %pad_maximum_fusion), channel_id=1, source_target_pairs={{0,1},{1,2},{2,3},{3,4},{4,5},{5,6},{6,7},{7,8},{8,9},{9,10},{10,1... | collective-permute-start | bytes 786440 | tf_op jit(solution)/shard_map/ppermute | solution.py:14
  30.1 0.6 fusion.93
  30.7 0.7 fusion.96
  31.3 5.7 %collective-permute-done = bf16[2,512,1,128]{3,1,2,0:T(8,128)(2,1)S(1)} collective-permute-done((bf16[2,512,1,128]{3,1,2,0:T(8,128)(2,1)S(1)}, bf16[2,512,1,128]{3,1,2,0:T(8,128)(2,1)S(1)}, u32[]{:S(2)}, u32[]{:S(2)}) %collective-permute-start) | collective-permute-done | bytes 262176 | tf_op jit(solution)/shard_map/ppermute | solution.py:14
  37.1 3.5 %collective-permute-start.1 = (bf16[2,512,1,128]{3,1,2,0:T(8,128)(2,1)S(1)}, bf16[2,512,1,128]{3,1,2,0:T(8,128)(2,1)S(1)}, u32[]{:S(2)}, u32[]{:S(2)}) collective-permute-start(bf16[2,512,1,128]{3,1,2,0:T(8,128)(2,1)S(1)} %collective-permute-done), channel_id=1, source_target_pairs={{0,1},{1,2},{2,3},{3,4},{4,5},{5,6},{6,7},{7,8},{8,9},{9,10},{10,1... | collective-permute-start | bytes 786440 | tf_op jit(solution)/shard_map/ppermute | solution.py:14
  45.5 0.6 slice.94
  49.7 0.5 slice.98
  51.4 0.6 fusion.94
  54.5 0.5 slice.101
  58.6 0.6 slice.104
  61.6 0.0 collective-permute-done.1
  61.7 3.2 %collective-permute-start.2 = (bf16[2,512,1,128]{3,1,2,0:T(8,128)(2,1)S(1)}, bf16[2,512,1,128]{3,1,2,0:T(8,128)(2,1)}, u32[]{:S(2)}, u32[]{:S(2)}) collective-permute-start(bf16[2,512,1,128]{3,1,2,0:T(8,128)(2,1)S(1)} %collective-permute-done.1), channel_id=1, source_target_pairs={{0,1},{1,2},{2,3},{3,4},{4,5},{5,6},{6,7},{7,8},{8,9},{9,10},{10,1... | collective-permute-start | bytes 786440 | tf_op jit(solution)/shard_map/ppermute | solution.py:14
  64.9 0.8 compare_and_fusion.2
  65.7 6.2 %collective-permute-done.2 = bf16[2,512,1,128]{3,1,2,0:T(8,128)(2,1)} collective-permute-done((bf16[2,512,1,128]{3,1,2,0:T(8,128)(2,1)S(1)}, bf16[2,512,1,128]{3,1,2,0:T(8,128)(2,1)}, u32[]{:S(2)}, u32[]{:S(2)}) %collective-permute-start.2) | collective-permute-done | bytes 262176 | tf_op jit(solution)/shard_map/ppermute | solution.py:14
  71.9 2.6 %collective-permute-start.3 = (bf16[2,512,1,128]{3,1,2,0:T(8,128)(2,1)}, bf16[2,512,1,128]{3,1,2,0:T(8,128)(2,1)}, u32[]{:S(2)}, u32[]{:S(2)}) collective-permute-start(bf16[2,512,1,128]{3,1,2,0:T(8,128)(2,1)} %collective-permute-done.2), channel_id=1, source_target_pairs={{0,1},{1,2},{2,3},{3,4},{4,5},{5,6},{6,7},{7,8},{8,9},{9,10},{10,1... | collective-permute-start | bytes 786440 | tf_op jit(solution)/shard_map/ppermute | solution.py:14
  74.5 0.7 slice_bitcast_fusion.2
  75.2 0.7 slice_bitcast_fusion
  75.8 0.0 all-to-all-done.1
  75.8 0.0 copy-start
  75.8 1.3 copy-done
  77.2 1.8 %copy.24 = bf16[8,64,16,128]{3,1,0,2:T(8,128)(2,1)S(1)} copy(bf16[8,64,16,128]{3,1,2,0:T(8,128)(2,1)} %bitcast.307) | data formatting | bytes 4194304 | tf_op jit(solution)/shard_map/all_to_all | solution.py:63
  79.0 14.0 %conditional.5 = (f32[512,1,16]{0,2,1:T(8,128)S(1)}, f32[512,1,16]{0,2,1:T(8,128)S(1)}, f32[512,1,16,128]{3,0,2,1:T(8,128)}) conditional(s32[]{:T(128)} %bitcast.79, () %tuple.38, (pred[512,512]{0,1:T(8,128)(4,1)S(1)}, bf16[512,1,128]{2,0,1:T(8,128)(2,1)S(1)}, bf16[512,1,16,128]{3,0,2,1:T(8,128)(2,1)S(1)}, bf16[512,1,128]{2,0,1:T(8,128)(2,1)S(1)}) %tuple.99), branch_computations={%region_0.0_spmd, %region_1.4_spmd} | conditional | flops 2203099136 | bytes 58064920 | solution.py:55
  79.0 3.2 %fusion = (f32[512,16]{0,1:T(8,128)S(1)}, f32[512,512,16]{1,0,2:T(8,128)S(1)}) fusion(pred[512,512]{0,1:T(8,128)(4,1)S(1)} %get-tuple-element.129, bf16[512,1,16,128]{3,0,2,1:T(8,128)(2,1)S(1)} %get-tuple-element.131, bf16[512,1,128]{2,0,1:T(8,128)(2,1)S(1)} %get-tuple-element.130), kind=kOutput, calls=%fused_computation.2 | convolution fusion | flops 1086316544 | bytes 19300352 | tf_op jit(solution)/shard_map/cond/branch_1_fun/tghd,sgd->tghs/dot_general | solution.py:21
  82.2 4.0 %fusion.2 = f32[512,16]{0,1:T(8,128)S(1)} fusion(f32[512,512,16]{1,0,2:T(8,128)S(1)} %get-tuple-element.213, f32[512,16]{0,1:T(8,128)S(1)} %get-tuple-element.211, pred[512,512]{0,1:T(8,128)(4,1)S(1)} %get-tuple-element.129), kind=kLoop, calls=%fused_computation.4 | loop fusion | flops 20963328 | bytes 17104896 | tf_op jit(solution)/shard_map/cond/branch_1_fun/reduce_sum | solution.py:29
  86.3 6.7 %fusion.7 = f32[512,1,16,128]{3,0,2,1:T(8,128)} fusion(f32[512,512,16]{1,0,2:T(8,128)S(1)} %get-tuple-element.213, f32[512,16]{0,1:T(8,128)S(1)} %get-tuple-element.211, pred[512,512]{0,1:T(8,128)(4,1)S(1)} %get-tuple-element.129, f32[512,16]{0,1:T(8,128)S(1)} %get-tuple-element.210, bf16[512,1,128]{2,0,1:T(8,128)(2,1)S(1)} %get-tuple-element.132), kind=kOutput, calls=%fused_computation.9 | convolution fusion | flops 1095761920 | bytes 21430272 | tf_op jit(solution)/shard_map/cond/branch_1_fun/tghs,sgd->tghd/dot_general | solution.py:30
  93.0 0.0 copy-start.1
  93.0 15.5 %conditional.6 = ((f32[512,1,16]{0,2,1:T(8,128)S(1)}, f32[512,1,16]{0,2,1:T(8,128)S(1)}, f32[512,1,16,128]{3,0,2,1:T(8,128)})) conditional(s32[]{:T(128)} %bitcast.78, (f32[512,1,16]{0,2,1:T(8,128)S(1)}, f32[512,1,16]{0,2,1:T(8,128)S(1)}, f32[512,1,16,128]{3,0,2,1:T(8,128)}) %conditional.5, (pred[512,512]{0,1:T(8,128)(4,1)S(1)}, ...), branch_computations={%region_4.5_spmd, %region_5.8_spmd} | conditional | flops 2204131328 | bytes 62914620 | solution.py:55
  93.0 0.0 copy-start.2
  93.0 3.2 %fusion.18 = (f32[512,16]{0,1:T(8,128)S(1)}, f32[512,512,16]{1,0,2:T(8,128)S(1)}) fusion(pred[512,512]{0,1:T(8,128)(4,1)S(1)} %get-tuple-element.134, bf16[512,1,16,128]{3,0,2,1:T(8,128)(2,1)S(1)} %get-tuple-element.136, bf16[512,1,128]{2,0,1:T(8,128)(2,1)S(1)} %get-tuple-element.135), kind=kOutput, calls=%fused_computation.23 | convolution fusion | flops 1086316544 | bytes 19300352 | tf_op jit(solution)/shard_map/cond/branch_1_fun/tghd,sgd->tghs/dot_general | solution.py:21
  96.2 4.0 %fusion.20 = f32[512,16]{0,1:T(8,128)S(1)} fusion(f32[512,512,16]{1,0,2:T(8,128)S(1)} %get-tuple-element.215, f32[512,16]{0,1:T(8,128)S(1)} %bitcast.313, pred[512,512]{0,1:T(8,128)(4,1)S(1)} %get-tuple-element.134), kind=kLoop, calls=%fused_computation.25 | loop fusion | flops 20963328 | bytes 17104896 | tf_op jit(solution)/shard_map/cond/branch_1_fun/reduce_sum | solution.py:29
  100.3 0.0 copy-done.2
  100.3 8.2 %bitcast_add_fusion.2 = f32[512,1,16,128]{3,0,2,1:T(8,128)} fusion(f32[512,1,16,128]{3,0,2,1:T(8,128)} %get-tuple-element.138, f32[512,512,16]{1,0,2:T(8,128)S(1)} %get-tuple-element.215, f32[512,16]{0,1:T(8,128)S(1)} %bitcast.314, pred[512,512]{0,1:T(8,128)(4,1)S(1)} %get-tuple-element.134, f32[512,16]{0,1:T(8,128)S(1)} %get-tuple-element.200, ...), kind=kOutput, calls=%fused_computation.29 | convolution fusion | flops 1096810496 | bytes 25624576 | tf_op jit(solution)/shard_map/cond/branch_1_fun/tghs,sgd->tghd/dot_general | solution.py:30
  108.5 0.0 copy-done.1
  108.5 15.5 %conditional.7 = ((f32[512,1,16]{0,2,1:T(8,128)S(1)}, f32[512,1,16]{0,2,1:T(8,128)S(1)}, f32[512,1,16,128]{3,0,2,1:T(8,128)})) conditional(s32[]{:T(128)} %bitcast.77, (f32[512,1,16]{0,2,1:T(8,128)S(1)}, f32[512,1,16]{0,2,1:T(8,128)S(1)}, f32[512,1,16,128]{3,0,2,1:T(8,128)}) %get-tuple-element.278, (pred[512,512]{0,1:T(8,128)(4,1)S(1)}, ...), branch_computations={%region_8.9_spmd, %region_9.12_spmd} | conditional | flops 2204131328 | bytes 62390304 | solution.py:55
  108.5 3.2 %fusion.35 = (f32[512,16]{0,1:T(8,128)S(1)}, f32[512,512,16]{1,0,2:T(8,128)S(1)}) fusion(pred[512,512]{0,1:T(8,128)(4,1)S(1)} %get-tuple-element.141, bf16[512,1,16,128]{3,0,2,1:T(8,128)(2,1)S(1)} %get-tuple-element.143, bf16[512,1,128]{2,0,1:T(8,128)(2,1)S(1)} %get-tuple-element.142), kind=kOutput, calls=%fused_computation.43 | convolution fusion | flops 1086316544 | bytes 19300352 | tf_op jit(solution)/shard_map/cond/branch_1_fun/tghd,sgd->tghs/dot_general | solution.py:21
  111.7 4.0 %fusion.37 = f32[512,16]{0,1:T(8,128)S(1)} fusion(f32[512,512,16]{1,0,2:T(8,128)S(1)} %get-tuple-element.217, f32[512,16]{0,1:T(8,128)S(1)} %bitcast.315, pred[512,512]{0,1:T(8,128)(4,1)S(1)} %get-tuple-element.141), kind=kLoop, calls=%fused_computation.45 | loop fusion | flops 20963328 | bytes 17104896 | tf_op jit(solution)/shard_map/cond/branch_1_fun/reduce_sum | solution.py:29
  115.8 8.2 %bitcast_add_fusion.4 = f32[512,1,16,128]{3,0,2,1:T(8,128)} fusion(f32[512,1,16,128]{3,0,2,1:T(8,128)} %get-tuple-element.145, f32[512,512,16]{1,0,2:T(8,128)S(1)} %get-tuple-element.217, f32[512,16]{0,1:T(8,128)S(1)} %bitcast.316, pred[512,512]{0,1:T(8,128)(4,1)S(1)} %get-tuple-element.141, f32[512,16]{0,1:T(8,128)S(1)} %get-tuple-element.202, ...), kind=kOutput, calls=%fused_computation.49 | convolution fusion | flops 1096810496 | bytes 25624576 | tf_op jit(solution)/shard_map/cond/branch_1_fun/tghs,sgd->tghd/dot_general | solution.py:30
  124.0 0.1 eq.26
  124.1 1.1 le.118
  125.2 17.5 %conditional.8 = ((f32[512,1,16]{0,2,1:T(8,128)S(1)}, f32[512,1,16]{0,2,1:T(8,128)S(1)}, f32[512,1,16,128]{3,0,2,1:T(8,128)})) conditional(s32[]{:T(128)} %bitcast.76, (f32[512,1,16]{0,2,1:T(8,128)S(1)}, f32[512,1,16]{0,2,1:T(8,128)S(1)}, f32[512,1,16,128]{3,0,2,1:T(8,128)}) %get-tuple-element.279, (s32[512]{0:T(512)S(1)}, ...), branch_computations={%region_12.13_spmd, %region_13.16_spmd} | conditional | flops 2204918272 | bytes 64757796 | solution.py:55
  125.2 1.5 compare_and_fusion
  126.7 3.7 %fusion.52 = (f32[512,16]{0,1:T(8,128)S(1)}, f32[512,512,16]{1,0,2:T(8,128)S(1)}) fusion(pred[512,512]{0,1:T(8,128)(4,1)S(1)} %compare_and_fusion, bf16[512,1,16,128]{3,0,2,1:T(8,128)(2,1)S(1)} %get-tuple-element.154, bf16[2,512,1,128]{3,1,2,0:T(8,128)(2,1)} %get-tuple-element.153), kind=kOutput, calls=%fused_computation.63 | convolution fusion | flops 1086316544 | bytes 19300352 | tf_op jit(solution)/shard_map/cond/branch_1_fun/tghd,sgd->tghs/dot_general | solution.py:21
  130.4 4.0 %fusion.54 = f32[512,16]{0,1:T(8,128)S(1)} fusion(f32[512,512,16]{1,0,2:T(8,128)S(1)} %get-tuple-element.219, f32[512,16]{0,1:T(8,128)S(1)} %bitcast.311, pred[512,512]{0,1:T(8,128)(4,1)S(1)} %compare_and_fusion), kind=kLoop, calls=%fused_computation.65 | loop fusion | flops 20963328 | bytes 17104896 | tf_op jit(solution)/shard_map/cond/branch_1_fun/reduce_sum | solution.py:29
  134.5 8.2 %bitcast_add_fusion.6 = f32[512,1,16,128]{3,0,2,1:T(8,128)} fusion(f32[512,1,16,128]{3,0,2,1:T(8,128)} %get-tuple-element.156, f32[512,512,16]{1,0,2:T(8,128)S(1)} %get-tuple-element.219, f32[512,16]{0,1:T(8,128)S(1)} %bitcast.312, pred[512,512]{0,1:T(8,128)(4,1)S(1)} %compare_and_fusion, f32[512,16]{0,1:T(8,128)S(1)} %get-tuple-element.204, ...), kind=kOutput, calls=%fused_computation.69 | convolution fusion | flops 1096810496 | bytes 25624576 | tf_op jit(solution)/shard_map/cond/branch_1_fun/tghs,sgd->tghd/dot_general | solution.py:30
  142.7 0.0 collective-permute-done.3
  142.7 20.9 %conditional.9 = (f32[512,1,16]{0,2,1:T(8,128)S(1)}, f32[512,1,16,128]{3,2,0,1:T(8,128)}) conditional(s32[]{:T(128)} %bitcast.75, (f32[512,1,16]{0,2,1:T(8,128)S(1)}, f32[512,1,16,128]{3,0,2,1:T(8,128)}) %tuple.43, (s32[512]{0:T(512)S(1)}, s32[512,512]{0,1:T(8,128)S(1)}, s32[]{:T(128)}, s32[1,512]{1,0:T(1,128)S(1)}, s32[512,512]{0,1:T(8,128)}, ...), branch_computations={%region_16.17_spmd, %region_17.20_spmd} | conditional | flops 2204918272 | bytes 73080848 | solution.py:55
  143.0 1.5 compare_and_fusion.1
  144.5 3.7 %fusion.71 = (f32[512,16]{0,1:T(8,128)S(1)}, f32[512,512,16]{1,0,2:T(8,128)S(1)}) fusion(pred[512,512]{0,1:T(8,128)(4,1)S(1)} %compare_and_fusion.1, bf16[512,1,16,128]{3,0,2,1:T(8,128)(2,1)S(1)} %get-tuple-element.165, bf16[2,512,1,128]{3,1,2,0:T(8,128)(2,1)} %get-tuple-element.164), kind=kOutput, calls=%fused_computation.87 | convolution fusion | flops 1086316544 | bytes 19300352 | tf_op jit(solution)/shard_map/cond/branch_1_fun/tghd,sgd->tghs/dot_general | solution.py:21
  148.2 4.0 %fusion.73 = f32[512,16]{0,1:T(8,128)S(1)} fusion(f32[512,512,16]{1,0,2:T(8,128)S(1)} %get-tuple-element.209, f32[512,16]{0,1:T(8,128)S(1)} %fusion.86, pred[512,512]{0,1:T(8,128)(4,1)S(1)} %compare_and_fusion.1), kind=kLoop, calls=%fused_computation.89 | loop fusion | flops 20963328 | bytes 17104896 | tf_op jit(solution)/shard_map/cond/branch_1_fun/reduce_sum | solution.py:29
  152.3 7.0 %bitcast_add_fusion.8 = f32[512,1,16,128]{3,0,2,1:T(8,128)S(1)} fusion(f32[512,1,16,128]{3,0,2,1:T(8,128)} %get-tuple-element.166, f32[512,512,16]{1,0,2:T(8,128)S(1)} %get-tuple-element.209, f32[512,16]{0,1:T(8,128)S(1)} %fusion.86, pred[512,512]{0,1:T(8,128)(4,1)S(1)} %compare_and_fusion.1, f32[512,16]{0,1:T(8,128)S(1)} %get-tuple-element.206, ...), kind=kOutput, calls=%fused_computation.93 | convolution fusion | flops 1096810496 | bytes 25624576 | tf_op jit(solution)/shard_map/cond/branch_1_fun/tghs,sgd->tghd/dot_general | solution.py:30
  159.3 4.4 %copy.34 = f32[512,1,16,128]{3,2,0,1:T(8,128)} copy(f32[512,1,16,128]{3,0,2,1:T(8,128)S(1)} %bitcast_add_fusion.8) | data formatting | bytes 8388608 | tf_op jit(solution)/shard_map/cond | solution.py:55
  163.7 0.1 copy.26
  163.8 3.8 %fusion.91 = bf16[512,16,128]{2,1,0:T(8,128)(2,1)} fusion(f32[512,1,16,128]{3,2,0,1:T(8,128)} %get-tuple-element.197, f32[512,16]{1,0:T(8,128)S(1)} %copy.26), kind=kLoop, calls=%fused_computation.111 | loop fusion | flops 2097152 | bytes 6324224 | tf_op jit(solution)/shard_map/reshape | solution.py:97
  (22 shorter events, 0.2 us)
Async XLA Ops:
  1.6 10.4 %all-to-all-start = ((bf16[64,8,128]{2,0,1:T(8,128)(2,1)}), bf16[64,8,128]{2,0,1:T(8,128)(2,1)S(1)}, u32[]{:S(2)}, u32[]{:S(2)}) async-start(bf16[64,8,128]{2,0,1:T(8,128)(2,1)} %copy.22), calls=%async_computation | async-start | bytes 262144 | tf_op jit(solution)/shard_map/all_to_all | solution.py:64
  12.0 9.4 %all-to-all-start.2 = ((bf16[64,8,128]{2,0,1:T(8,128)(2,1)}), bf16[64,8,128]{2,0,1:T(8,128)(2,1)S(1)}, u32[]{:S(2)}, u32[]{:S(2)}) async-start(bf16[64,8,128]{2,0,1:T(8,128)(2,1)} %copy.25), calls=%async_computation.2 | async-start | bytes 262144 | tf_op jit(solution)/shard_map/all_to_all | solution.py:65
  21.4 54.5 %all-to-all-start.1 = ((bf16[64,128,128]{2,0,1:T(8,128)(2,1)}), bf16[64,128,128]{2,0,1:T(8,128)(2,1)S(1)}, u32[]{:S(2)}, u32[]{:S(2)}) async-start(bf16[64,128,128]{2,0,1:T(8,128)(2,1)} %copy.23), calls=%async_computation.1 | async-start | bytes 4194304 | tf_op jit(solution)/shard_map/all_to_all | solution.py:63
  26.6 10.5 %collective-permute-start = (bf16[2,512,1,128]{3,1,2,0:T(8,128)(2,1)S(1)}, bf16[2,512,1,128]{3,1,2,0:T(8,128)(2,1)S(1)}, u32[]{:S(2)}, u32[]{:S(2)}) collective-permute-start(bf16[2,512,1,128]{3,1,2,0:T(8,128)(2,1)S(1)} %pad_maximum_fusion), channel_id=1, source_target_pairs={{0,1},{1,2},{2,3},{3,4},{4,5},{5,6},{6,7},{7,8},{8,9},{9,10},{10,1... | collective-permute-start | bytes 786440 | tf_op jit(solution)/shard_map/ppermute | solution.py:14
  37.1 24.6 %collective-permute-start.1 = (bf16[2,512,1,128]{3,1,2,0:T(8,128)(2,1)S(1)}, bf16[2,512,1,128]{3,1,2,0:T(8,128)(2,1)S(1)}, u32[]{:S(2)}, u32[]{:S(2)}) collective-permute-start(bf16[2,512,1,128]{3,1,2,0:T(8,128)(2,1)S(1)} %collective-permute-done), channel_id=1, source_target_pairs={{0,1},{1,2},{2,3},{3,4},{4,5},{5,6},{6,7},{7,8},{8,9},{9,10},{10,1... | collective-permute-start | bytes 786440 | tf_op jit(solution)/shard_map/ppermute | solution.py:14
  61.7 10.2 %collective-permute-start.2 = (bf16[2,512,1,128]{3,1,2,0:T(8,128)(2,1)S(1)}, bf16[2,512,1,128]{3,1,2,0:T(8,128)(2,1)}, u32[]{:S(2)}, u32[]{:S(2)}) collective-permute-start(bf16[2,512,1,128]{3,1,2,0:T(8,128)(2,1)S(1)} %collective-permute-done.1), channel_id=1, source_target_pairs={{0,1},{1,2},{2,3},{3,4},{4,5},{5,6},{6,7},{7,8},{8,9},{9,10},{10,1... | collective-permute-start | bytes 786440 | tf_op jit(solution)/shard_map/ppermute | solution.py:14
  71.9 70.9 %collective-permute-start.3 = (bf16[2,512,1,128]{3,1,2,0:T(8,128)(2,1)}, bf16[2,512,1,128]{3,1,2,0:T(8,128)(2,1)}, u32[]{:S(2)}, u32[]{:S(2)}) collective-permute-start(bf16[2,512,1,128]{3,1,2,0:T(8,128)(2,1)} %collective-permute-done.2), channel_id=1, source_target_pairs={{0,1},{1,2},{2,3},{3,4},{4,5},{5,6},{6,7},{7,8},{8,9},{9,10},{10,1... | collective-permute-start | bytes 786440 | tf_op jit(solution)/shard_map/ppermute | solution.py:14
  75.8 1.3 copy-start
  93.0 15.5 %copy-start.1 = (bf16[512,1,128]{2,0,1:T(8,128)(2,1)S(1)}, bf16[512,1,128]{2,0,1:T(8,128)(2,1)}, u32[]{:S(2)}) copy-start(bf16[512,1,128]{2,0,1:T(8,128)(2,1)} %get-tuple-element.220) | copy-start | bytes 393220
  93.0 7.3 %copy-start.2 = (bf16[512,1,128]{2,0,1:T(8,128)(2,1)S(1)}, bf16[512,1,128]{2,0,1:T(8,128)(2,1)}, u32[]{:S(2)}) copy-start(bf16[512,1,128]{2,0,1:T(8,128)(2,1)} %get-tuple-element.139) | copy-start | bytes 393220 | tf_op jit(solution)/shard_map/cond
where the time goes:
time: 169 us; the launch traced here: 168 us
  matrix products  55.3 us (33%)
  other arithmetic  28.9 us (17%)
  starting transfers between devices  24.1 us (14%)
  local copies, waits for them, and re-layouts  22.3 us (13%)
  between operations  18.5 us (11%)
  waiting for transfers between devices  18.2 us (11%)
    dot_general x5, matrix products, update_carried(): jnp.einsum('tghs,sgd->tghd', weights.astype(jnp.bfloat16), value_tile, pr...  38.4 us
    reduce_sum x5, other arithmetic, update_carried(): new_sum = run_sum * factor + jnp.sum(weights, axis=-1)  20 us
    dot_general x5, matrix products, update_carried(): jnp.einsum('tghd,sgd->tghs', grouped_q, key_tile, preferred_element_type=...  16.9 us
    ppermute x4, starting transfers between devices, from_behind(): return lax.ppermute(block, axis, route)  12.8 us
    ppermute x4, waiting for transfers between devices, from_behind(): return lax.ppermute(block, axis, route)  11.9 us
    unnamed x7, local copies, waits for them, and re-layouts  8.74 us
    all_to_all x1, waiting for transfers between devices, per_device(): lax.all_to_all(keys, 'head', split_axis=1, concat_axis=0, tiled=True)  4.53 us
    cond x1, local copies, waits for them, and re-layouts, attend_span(): carried = lax.cond(needed, run_block, keep_carried, carried)  4.4 us
  transfers between devices with their start and end apart: 7, of which 4 were waited for; matrix products, arithmetic and copies ran while one was open for 47% of the time, Pallas kernels for 0%

commit v1 on v0

v1 whole, which is shorter than its diff:
```python
import functools
import math

import jax
import jax.numpy as jnp
from jax import lax
from jax.experimental import pallas as pl
from jax.experimental.pallas import tpu as pltpu
from jax.sharding import PartitionSpec as P

MESH = pl.DeviceIdType.MESH
REACH = 4
BLOCK = 512
PIECE = 64
CHUNK = 128
HEADS = 16
WIDTH = 128
WINDOW = REACH * BLOCK + CHUNK
TILE = 32
ROWS = TILE * HEADS
DOCS = 32
PENALTY = 32768.0
SCALE = math.log2(math.e) / math.sqrt(WIDTH)
PEERS = [(0, 1), (1, 0), (1, 1), (3, 0), (3, 1), (2, 0), (2, 1)]


def kernel(q_hbm, kv_hbm, doc_ref, out_hbm, kv, qb, ab, tab, sb, ob,
           kv_send, kv_recv, q_send, q_recv, seq_send, seq_recv, loc_sem, out_sem):
    head, seq = lax.axis_index("head"), lax.axis_index("seq")
    x, core = head // 2, head % 2

    def to(dx, dc):
        return 2 * ((x + dx) % 4) + (core + dc) % 2

    def came(dx, dc):
        return 2 * ((x - dx + 4) % 4) + (core + dc) % 2

    barrier = pltpu.get_barrier_semaphore()
    for dx, dc in PEERS:
        pl.semaphore_signal(barrier, inc=1, device_id={"head": to(dx, dc)}, device_id_type=MESH)
    for d in range(1, REACH + 1):
        pl.semaphore_signal(barrier, inc=1, device_id={"seq": (seq + 32 - d) % 32}, device_id_type=MESH)

    own_rows = pl.ds(pl.multiple_of(REACH * BLOCK + PIECE * head, PIECE), PIECE)
    own_kv = pltpu.make_async_copy(kv_hbm.at[head], kv.at[own_rows, 128:384], loc_sem.at[0])
    own_kv.start()
    own_q = pltpu.make_async_copy(
        q_hbm.at[:, pl.ds(pl.multiple_of(HEADS * head, HEADS), HEADS), :],
        qb.at[pl.ds(pl.multiple_of(PIECE * head, PIECE), PIECE)], loc_sem.at[1])
    own_q.start()
    pl.semaphore_wait(barrier, len(PEERS) + REACH)

    def kv_copy(dx, dc, sender):
        target = to(dx, dc)
        rows = pl.ds(pl.multiple_of(REACH * BLOCK + PIECE * sender, PIECE), PIECE)
        return pltpu.make_async_remote_copy(
            kv_hbm.at[target], kv.at[rows, 128:384],
            kv_send.at[2 * dx + dc], kv_recv.at[2 * dx + dc],
            device_id={"head": target}, device_id_type=MESH)

    def q_copy(dx, dc, sender):
        target = to(dx, dc)
        return pltpu.make_async_remote_copy(
            q_hbm.at[:, pl.ds(pl.multiple_of(HEADS * target, HEADS), HEADS), :],
            qb.at[pl.ds(pl.multiple_of(PIECE * sender, PIECE), PIECE)],
            q_send.at[2 * dx + dc], q_recv.at[2 * dx + dc],
            device_id={"head": target}, device_id_type=MESH)

    def seq_copy(d):
        return pltpu.make_async_remote_copy(
            kv.at[REACH * BLOCK:, 128:384],
            kv.at[(REACH - d) * BLOCK:(REACH - d + 1) * BLOCK, 128:384],
            seq_send.at[d - 1], seq_recv.at[d - 1],
            device_id={"seq": (seq + d) % 32}, device_id_type=MESH)

    for dx, dc in PEERS:
        kv_copy(dx, dc, head).start()
    for dx, dc in PEERS:
        q_copy(dx, dc, head).start()

    own_kv.wait()
    for dx, dc in PEERS:
        kv_copy(dx, dc, came(dx, dc)).wait_recv()
    for d in range(1, REACH + 1):
        seq_copy(d).start()

    lane = lax.broadcasted_iota(jnp.int32, (BLOCK, 128), 1)
    for b in range(REACH + 1):
        row = doc_ref[pl.ds((seq + 32 - REACH + b) % 32, 1), :]
        cols = jnp.broadcast_to(row, (128, BLOCK)).astype(jnp.float32).T.astype(jnp.int32)
        same = cols == lane
        kv[b * BLOCK:(b + 1) * BLOCK, 0:128] = jnp.where(same, 1.0, 0.0).astype(jnp.bfloat16)
        kv[b * BLOCK:(b + 1) * BLOCK, 384:512] = jnp.ones((BLOCK, 128), jnp.bfloat16)
        if b == REACH:
            tab[...] = jnp.where(same | (lane >= DOCS), 0.0, -PENALTY)

    def spread(i, _):
        rows = pl.ds(pl.multiple_of(16 * i, 16), 16)
        ab[rows] = jnp.broadcast_to(tab[rows, :][:, None, :], (16, HEADS, 128)).astype(jnp.bfloat16)
        return 0

    lax.fori_loop(0, BLOCK // 16, spread, 0)

    own_q.wait()
    q_copy(0, 1, came(0, 1)).wait_recv()
    for d in range(1, REACH + 1):
        seq_copy(d).wait_recv()

    tiles = CHUNK // TILE
    steps = 4 * tiles

    def place(t):
        order = t // tiles
        dx = order + jnp.where(order == 2, 1, 0) - jnp.where(order == 3, 1, 0)
        chunk = (x - dx + 4) % 4
        return chunk, dx, t % tiles

    def scores(t, slot):
        chunk, _, part = place(t)
        rows = pl.ds(pl.multiple_of(CHUNK * chunk + TILE * part, TILE), TILE)
        left = jnp.concatenate(
            [ab[rows].reshape(ROWS, WIDTH), qb[rows].reshape(ROWS, WIDTH)], axis=1)
        keys = kv[pl.ds(pl.multiple_of(CHUNK * chunk, CHUNK), WINDOW), 0:256]
        sb[slot] = lax.dot_general(
            left, keys, (((1,), (1,)), ((), ())), preferred_element_type=jnp.float32)

    def weigh(t, slot):
        chunk, _, part = place(t)
        token = lax.broadcasted_iota(jnp.int32, (ROWS, CHUNK), 0) // HEADS + TILE * part
        key = lax.broadcasted_iota(jnp.int32, (ROWS, CHUNK), 1)
        last = jnp.where(key <= token, sb[slot, :, WINDOW - CHUNK:], -PENALTY)
        s = jnp.concatenate([sb[slot, :, :WINDOW - CHUNK], last], axis=1)
        top = jnp.max(s, axis=1, keepdims=True)
        weights = jnp.exp2((s - top) * SCALE).astype(jnp.bfloat16)
        vals = kv[pl.ds(pl.multiple_of(CHUNK * chunk, CHUNK), WINDOW), 256:512]
        o = jnp.dot(weights, vals, preferred_element_type=jnp.float32)
        rows = pl.ds(pl.multiple_of(CHUNK * chunk + TILE * part, TILE), TILE)
        ob[rows] = (o[:, :128] / o[:, 128:]).astype(jnp.bfloat16).reshape(TILE, HEADS, WIDTH)

    def pair(j, _):
        t = 2 * j
        scores(t + 1, 1)
        weigh(t, 0)
        following = jnp.minimum(t + 2, steps - 1)

        @pl.when((following % tiles == 0) & (t + 2 < steps))
        def _():
            _, dx, _ = place(following)
            for dc in range(2):
                source = 2 * ((x - dx + 4) % 4) + (core + dc) % 2
                pltpu.make_async_remote_copy(
                    q_hbm.at[:, 0:HEADS, :],
                    qb.at[pl.ds(pl.multiple_of(PIECE * source, PIECE), PIECE)],
                    q_send.at[0], q_recv.at[2 * dx + dc],
                    device_id={"head": source}, device_id_type=MESH).wait_recv()

        scores(following, 0)
        weigh(t + 1, 1)
        return 0

    scores(jnp.int32(0), 0)
    lax.fori_loop(0, steps // 2, pair, 0)
    out = pltpu.make_async_copy(ob, out_hbm, out_sem)
    out.start()
    for dx, dc in PEERS:
        kv_copy(dx, dc, head).wait_send()
        q_copy(dx, dc, head).wait_send()
    for d in range(1, REACH + 1):
        seq_copy(d).wait_send()
    out.wait()


def per_device(queries, keys, values, doc_ids):
    kv = jnp.concatenate([keys, values], axis=-1).transpose(1, 0, 2)
    docs = doc_ids.reshape(32, BLOCK)
    hbm = pl.BlockSpec(memory_space=pl.ANY)
    dma = pltpu.SemaphoreType.DMA
    return pl.pallas_call(
        kernel,
        out_shape=jax.ShapeDtypeStruct((BLOCK, HEADS, WIDTH), jnp.bfloat16),
        in_specs=[hbm, hbm, pl.BlockSpec(memory_space=pltpu.VMEM)],
        out_specs=hbm,
        scratch_shapes=[
            pltpu.VMEM(((REACH + 1) * BLOCK, 512), jnp.bfloat16),
            pltpu.VMEM((BLOCK, HEADS, WIDTH), jnp.bfloat16),
            pltpu.VMEM((BLOCK, HEADS, WIDTH), jnp.bfloat16),
            pltpu.VMEM((BLOCK, 128), jnp.float32),
            pltpu.VMEM((2, ROWS, WINDOW), jnp.float32),
            pltpu.VMEM((BLOCK, HEADS, WIDTH), jnp.bfloat16),
            dma((8,)), dma((8,)), dma((8,)), dma((8,)), dma((4,)), dma((4,)), dma((2,)), dma,
        ],
        compiler_params=pltpu.CompilerParams(
            collective_id=0, has_side_effects=True, vmem_limit_bytes=56 << 20),
    )(queries, kv, docs)


def solution(mesh):
    spec = P(("seq", "head"), None, None)
    return jax.shard_map(
        per_device, mesh=mesh, in_specs=(spec, spec, spec, P()),
        out_specs=P("seq", "head", None), check_vma=False)
```

time: 169 us -> 81.1 us (0.48)
  the two profiles are of different devices: /device:TPU:136 before, /device:TPU:25 now
where the time goes in v1:
time: 81.1 us; the launch traced here: 80.8 us
  Pallas kernels  73.5 us (91%)
  local copies, waits for them, and re-layouts  6.59 us (8%)
    pallas_call x1, Pallas kernels, per_device(): pl.pallas_call(kernel, out_shape=jax.ShapeDtypeStruct((BLOCK, HEADS, WIDT...  73.5 us
    unnamed x3, local copies, waits for them, and re-layouts  5.12 us

profile of v1, /device:TPU:25, one launch (start us, length us, event | category | flops | bytes accessed | tf_op | source)
XLA Modules:
  0.0 80.8 jit_solution(663349005355737330)
XLA Ops:
  0.0 1.5 %reshape.3.doc_ref = s32[32,512]{1,0:T(8,128)} reshape(s32[16384]{0:T(1024)} %param.7) | data formatting | bytes 131072 | tf_op jit(solution)/shard_map/reshape | solution.py:175
  1.5 0.9 %copy.5 = bf16[64,8,128]{2,0,1:T(8,128)(2,1)S(1)} copy(bf16[64,8,128]{2,1,0:T(8,128)(2,1)} %param.5) | data formatting | bytes 262144 | tf_op args[1]
  2.4 0.9 %copy.6 = bf16[64,8,128]{2,0,1:T(8,128)(2,1)S(1)} copy(bf16[64,8,128]{2,1,0:T(8,128)(2,1)} %param.6) | data formatting | bytes 262144 | tf_op args[2]
  3.3 0.7 maximum_bitcast_fusion.kv_hbm
  4.1 73.5 %shard_map.46 = bf16[512,16,128]{2,1,0:T(8,128)(2,1)} custom-call(bf16[64,128,128]{2,1,0:T(8,128)(2,1)} %q_hbm.1, bf16[8,64,256]{2,1,0:T(8,128)(2,1)} %maximum_bitcast_fusion.kv_hbm, s32[32,512]{1,0:T(8,128)} %reshape.3.doc_ref), custom_call_target="tpu_custom_call" | custom-call | tf_op jit(solution)/shard_map/pallas_call | solution.py:178
  77.6 3.3 %copy.8 = bf16[512,16,128]{2,1,0:T(8,128)(2,1)} copy(bf16[512,16,128]{2,1,0:T(8,128)(2,1)} %shard_map.46) | data formatting | bytes 4194304

commit v2 on v1

--- a/solution.py
+++ b/solution.py
@@ -24,10 +24,11 @@
 PEERS = [(0, 1), (1, 0), (1, 1), (3, 0), (3, 1), (2, 0), (2, 1)]
 
 
-def kernel(q_hbm, kv_hbm, doc_ref, out_hbm, kv, qb, ab, tab, sb, ob,
-           kv_send, kv_recv, q_send, q_recv, seq_send, seq_recv, loc_sem, out_sem):
+def kernel(q_hbm, k_hbm, v_hbm, doc_hbm, ob, kin, vin, kvs, docs, kv, qb, ab, tab, sb,
+           kv_send, kv_recv, q_send, q_recv, seq_send, seq_recv, loc_sem, doc_sem):
     head, seq = lax.axis_index("head"), lax.axis_index("seq")
     x, core = head // 2, head % 2
+    y = seq % 4
 
     def to(dx, dc):
         return 2 * ((x + dx) % 4) + (core + dc) % 2
@@ -35,26 +36,39 @@
     def came(dx, dc):
         return 2 * ((x - dx + 4) % 4) + (core + dc) % 2
 
-    barrier = pltpu.get_barrier_semaphore()
-    for dx, dc in PEERS:
-        pl.semaphore_signal(barrier, inc=1, device_id={"head": to(dx, dc)}, device_id_type=MESH)
-    for d in range(1, REACH + 1):
-        pl.semaphore_signal(barrier, inc=1, device_id={"seq": (seq + 32 - d) % 32}, device_id_type=MESH)
-
-    own_rows = pl.ds(pl.multiple_of(REACH * BLOCK + PIECE * head, PIECE), PIECE)
-    own_kv = pltpu.make_async_copy(kv_hbm.at[head], kv.at[own_rows, 128:384], loc_sem.at[0])
-    own_kv.start()
+    k_in = pltpu.make_async_copy(k_hbm, kin, loc_sem.at[2])
+    v_in = pltpu.make_async_copy(v_hbm, vin, loc_sem.at[3])
+    k_in.start()
+    v_in.start()
+    doc_in = []
+    for b in range(REACH + 1):
+        start = pl.multiple_of((seq + 32 - REACH + b) % 32 * BLOCK, BLOCK)
+        doc_in.append(pltpu.make_async_copy(doc_hbm.at[pl.ds(start, BLOCK)], docs.at[b, 0], doc_sem.at[b]))
+        doc_in[-1].start()
     own_q = pltpu.make_async_copy(
         q_hbm.at[:, pl.ds(pl.multiple_of(HEADS * head, HEADS), HEADS), :],
         qb.at[pl.ds(pl.multiple_of(PIECE * head, PIECE), PIECE)], loc_sem.at[1])
     own_q.start()
-    pl.semaphore_wait(barrier, len(PEERS) + REACH)
+
+    barrier = pltpu.get_barrier_semaphore()
+    for dx, dc in PEERS:
+        pl.semaphore_signal(barrier, inc=1, device_id={"head": to(dx, dc)}, device_id_type=MESH)
+    up = (seq // 4) * 4 + (y + 1) % 4
+    down = (seq // 4) * 4 + (y + 3) % 4
+    for other in (up, down, (seq + 28) % 32):
+        pl.semaphore_signal(barrier, inc=1, device_id={"seq": other}, device_id_type=MESH)
+
+    k_in.wait()
+    v_in.wait()
+    kvs[:, :, 0:128] = jnp.transpose(kin[...], (1, 0, 2))
+    kvs[:, :, 128:256] = jnp.transpose(vin[...], (1, 0, 2))
+    pl.semaphore_wait(barrier, len(PEERS) + 3)
 
     def kv_copy(dx, dc, sender):
         target = to(dx, dc)
         rows = pl.ds(pl.multiple_of(REACH * BLOCK + PIECE * sender, PIECE), PIECE)
         return pltpu.make_async_remote_copy(
-            kv_hbm.at[target], kv.at[rows, 128:384],
+            kvs.at[target], kv.at[rows, 128:384],
             kv_send.at[2 * dx + dc], kv_recv.at[2 * dx + dc],
             device_id={"head": target}, device_id_type=MESH)
 
@@ -66,34 +80,98 @@
             q_send.at[2 * dx + dc], q_recv.at[2 * dx + dc],
             device_id={"head": target}, device_id_type=MESH)
 
-    def seq_copy(d):
+    own_rows = pl.ds(pl.multiple_of(REACH * BLOCK + PIECE * head, PIECE), PIECE)
+    own_kv = pltpu.make_async_copy(kvs.at[head], kv.at[own_rows, 128:384], loc_sem.at[0])
+    own_kv.start()
+    for dx, dc in PEERS:
+        kv_copy(dx, dc, head).start()
+    for dx, dc in PEERS:
+        q_copy(dx, dc, head).start()
+
+    def part(d, dx):
+        return pl.ds(pl.multiple_of(
+            (REACH - d) * BLOCK + CHUNK * ((x - dx + 4) % 4), CHUNK), CHUNK)
+
+    def pass_on(src, d, dx, target, lane):
         return pltpu.make_async_remote_copy(
-            kv.at[REACH * BLOCK:, 128:384],
-            kv.at[(REACH - d) * BLOCK:(REACH - d + 1) * BLOCK, 128:384],
-            seq_send.at[d - 1], seq_recv.at[d - 1],
-            device_id={"seq": (seq + d) % 32}, device_id_type=MESH)
-
-    for dx, dc in PEERS:
-        kv_copy(dx, dc, head).start()
-    for dx, dc in PEERS:
-        q_copy(dx, dc, head).start()
-
-    own_kv.wait()
-    for dx, dc in PEERS:
-        kv_copy(dx, dc, came(dx, dc)).wait_recv()
-    for d in range(1, REACH + 1):
-        seq_copy(d).start()
+            kv.at[part(src, dx), 128:384], kv.at[part(d, dx), 128:384],
+            seq_send.at[4 * lane + dx], seq_recv.at[4 * (d - 1) + dx],
+            device_id={"seq": target}, device_id_type=MESH)
+
+    def arrive(d, dx):
+        pass_on(d, d, dx, up, 0).wait_recv()
+
+    def own_part(dx):
+        if dx == 0:
+            own_kv.wait()
+        else:
+            kv_copy(dx, 0, came(dx, 0)).wait_recv()
+        kv_copy(dx, 1, came(dx, 1)).wait_recv()
+        pass_on(0, 4, dx, (seq + 4) % 32, 0).start()
+
+        @pl.when(y < 3)
+        def _():
+            pass_on(0, 1, dx, up, 1).start()
+
+        @pl.when(y == 0)
+        def _():
+            pass_on(0, 3, dx, down, 2).start()
+
+    def far_part(dx):
+        arrive(4, dx)
+
+        @pl.when(y > 0)
+        def _():
+            pass_on(4, 3, dx, down, 2).start()
+
+        @pl.when(y == 3)
+        def _():
+            pass_on(4, 1, dx, up, 1).start()
+
+    middle = (y == 1) | (y == 2)
+
+    def near_part(dx):
+        arrive(1, dx)
+
+        @pl.when(middle)
+        def _():
+            pass_on(1, 2, dx, up, 3).start()
+
+    def third_part(dx):
+        arrive(3, dx)
+
+        @pl.when(middle)
+        def _():
+            pass_on(3, 2, dx, down, 4).start()
 
     lane = lax.broadcasted_iota(jnp.int32, (BLOCK, 128), 1)
-    for b in range(REACH + 1):
-        row = doc_ref[pl.ds((seq + 32 - REACH + b) % 32, 1), :]
-        cols = jnp.broadcast_to(row, (128, BLOCK)).astype(jnp.float32).T.astype(jnp.int32)
+    for b in range(REACH, -1, -1):
+        doc_in[b].wait()
+        cols = jnp.broadcast_to(docs[b], (128, BLOCK)).astype(jnp.float32).T.astype(jnp.int32)
         same = cols == lane
         kv[b * BLOCK:(b + 1) * BLOCK, 0:128] = jnp.where(same, 1.0, 0.0).astype(jnp.bfloat16)
         kv[b * BLOCK:(b + 1) * BLOCK, 384:512] = jnp.ones((BLOCK, 128), jnp.bfloat16)
         if b == REACH:
             tab[...] = jnp.where(same | (lane >= DOCS), 0.0, -PENALTY)
 
+    D = [0, 1, 3, 2]
+    own_part(D[0])
+    own_part(D[1])
+    far_part(D[0])
+    near_part(D[0])
+    own_part(D[2])
+    far_part(D[1])
+    near_part(D[1])
+    third_part(D[0])
+    own_part(D[3])
+    far_part(D[2])
+    near_part(D[2])
+    third_part(D[1])
+    far_part(D[3])
+    near_part(D[3])
+    third_part(D[2])
+    third_part(D[3])
+
     def spread(i, _):
         rows = pl.ds(pl.multiple_of(16 * i, 16), 16)
         ab[rows] = jnp.broadcast_to(tab[rows, :][:, None, :], (16, HEADS, 128)).astype(jnp.bfloat16)
@@ -103,8 +181,8 @@
 
     own_q.wait()
     q_copy(0, 1, came(0, 1)).wait_recv()
-    for d in range(1, REACH + 1):
-        seq_copy(d).wait_recv()
+    for dx in D:
+        arrive(2, dx)
 
     tiles = CHUNK // TILE
     steps = 4 * tiles
@@ -160,38 +238,43 @@
 
     scores(jnp.int32(0), 0)
     lax.fori_loop(0, steps // 2, pair, 0)
-    out = pltpu.make_async_copy(ob, out_hbm, out_sem)
-    out.start()
     for dx, dc in PEERS:
         kv_copy(dx, dc, head).wait_send()
         q_copy(dx, dc, head).wait_send()
-    for d in range(1, REACH + 1):
-        seq_copy(d).wait_send()
-    out.wait()
+    for dx in D:
+        pass_on(0, 4, dx, (seq + 4) % 32, 0).wait_send()
+        pass_on(0, 1, dx, up, 1).wait_send()
+        pass_on(0, 3, dx, down, 2).wait_send()
+
+        @pl.when(middle)
+        def _():
+            pass_on(1, 2, dx, up, 3).wait_send()
+            pass_on(3, 2, dx, down, 4).wait_send()
 
 
 def per_device(queries, keys, values, doc_ids):
-    kv = jnp.concatenate([keys, values], axis=-1).transpose(1, 0, 2)
-    docs = doc_ids.reshape(32, BLOCK)
-    hbm = pl.BlockSpec(memory_space=pl.ANY)
+    hbm = pl.BlockSpec(memory_space=pltpu.HBM)
     dma = pltpu.SemaphoreType.DMA
     return pl.pallas_call(
         kernel,
         out_shape=jax.ShapeDtypeStruct((BLOCK, HEADS, WIDTH), jnp.bfloat16),
-        in_specs=[hbm, hbm, pl.BlockSpec(memory_space=pltpu.VMEM)],
-        out_specs=hbm,
+        in_specs=[hbm] * 4,
+        out_specs=pl.BlockSpec(memory_space=pltpu.VMEM),
         scratch_shapes=[
+            pltpu.VMEM((PIECE, 8, WIDTH), jnp.bfloat16),
+            pltpu.VMEM((PIECE, 8, WIDTH), jnp.bfloat16),
+            pltpu.VMEM((8, PIECE, 2 * WIDTH), jnp.bfloat16),
+            pltpu.VMEM((8, 1, BLOCK), jnp.int32),
             pltpu.VMEM(((REACH + 1) * BLOCK, 512), jnp.bfloat16),
             pltpu.VMEM((BLOCK, HEADS, WIDTH), jnp.bfloat16),
             pltpu.VMEM((BLOCK, HEADS, WIDTH), jnp.bfloat16),
             pltpu.VMEM((BLOCK, 128), jnp.float32),
             pltpu.VMEM((2, ROWS, WINDOW), jnp.float32),
-            pltpu.VMEM((BLOCK, HEADS, WIDTH), jnp.bfloat16),
-            dma((8,)), dma((8,)), dma((8,)), dma((8,)), dma((4,)), dma((4,)), dma((2,)), dma,
+            dma((8,)), dma((8,)), dma((8,)), dma((8,)), dma((20,)), dma((16,)), dma((4,)), dma((5,)),
         ],
         compiler_params=pltpu.CompilerParams(
-            collective_id=0, has_side_effects=True, vmem_limit_bytes=56 << 20),
-    )(queries, kv, docs)
+            collective_id=0, has_side_effects=True, vmem_limit_bytes=30 << 20),
+    )(*(pltpu.with_memory_space_constraint(v, pltpu.HBM) for v in (queries, keys, values, doc_ids)))
 
 
 def solution(mesh):

time: 81.1 us -> 58.3 us (0.72)
  the two profiles are of different devices: /device:TPU:25 before, /device:TPU:1 now
where the time goes in v2:
time: 58.3 us; the launch traced here: 58.2 us
  Pallas kernels  56.9 us (98%)
  local copies, waits for them, and re-layouts  1.32 us (2%)
    pallas_call x1, Pallas kernels, per_device(): pl.pallas_call(kernel, out_shape=jax.ShapeDtypeStruct((BLOCK, HEADS, WIDT...  56.9 us
    unnamed x1, local copies, waits for them, and re-layouts  1.32 us

profile of v2, /device:TPU:1, one launch (start us, length us, event | category | flops | bytes accessed | tf_op | source)
XLA Modules:
  0.0 58.2 jit_solution(2026108713733899044)
XLA Ops:
  0.0 56.9 %shard_map.46 = bf16[512,16,128]{2,1,0:T(8,128)(2,1)S(1)} custom-call(bf16[64,128,128]{2,1,0:T(8,128)(2,1)} %q_hbm.1, bf16[64,8,128]{2,1,0:T(8,128)(2,1)} %k_hbm.1, bf16[64,8,128]{2,1,0:T(8,128)(2,1)} %v_hbm.1, s32[16384]{0:T(1024)} %doc_hbm.1), custom_call_target="tpu_custom_call" | custom-call | tf_op jit(solution)/shard_map/pallas_call | solution.py:258
  56.9 1.3 %copy.6 = bf16[512,16,128]{2,1,0:T(8,128)(2,1)} copy(bf16[512,16,128]{2,1,0:T(8,128)(2,1)S(1)} %shard_map.46) | data formatting | bytes 4194304

commit v3 on v2

v3 whole, which is shorter than its diff:
```python
import functools
import math

import jax
import jax.numpy as jnp
from jax import lax
from jax.experimental import pallas as pl
from jax.experimental.pallas import tpu as pltpu
from jax.sharding import PartitionSpec as P

MESH = pl.DeviceIdType.MESH
REACH = 4
BLOCK = 512
PIECE = 64
CHUNK = 128
HEADS = 16
WIDTH = 128
WINDOW = REACH * BLOCK + CHUNK
TILE = 32
ROWS = TILE * HEADS
DOCS = 32
PENALTY = 32768.0
SCALE = math.log2(math.e) / math.sqrt(WIDTH)
ORDER = [(0, 0), (0, 1), (1, 0), (3, 0), (1, 1), (3, 1), (2, 0), (2, 1)]
PEERS = ORDER[1:]
PARTS = [0, 1, 3, 2]
EARLY = 8


def kernel(q_hbm, k_hbm, v_hbm, doc_hbm, ob, kin, vin, kvs, docs, kv, qb, ab, tab, sb, acc, tops,
           kv_send, kv_recv, q_send, q_recv, seq_send, seq_recv, loc_sem, doc_sem):
    head, seq = lax.axis_index("head"), lax.axis_index("seq")
    x, core = head // 2, head % 2
    y = seq % 4
    behind = seq >= 4
    middle = (y == 1) | (y == 2)

    def to(dx, dc):
        return 2 * ((x + dx) % 4) + (core + dc) % 2

    def came(dx, dc):
        return 2 * ((x - dx + 4) % 4) + (core + dc) % 2

    k_in = pltpu.make_async_copy(k_hbm, kin, loc_sem.at[2])
    v_in = pltpu.make_async_copy(v_hbm, vin, loc_sem.at[3])
    k_in.start()
    v_in.start()
    doc_in = []
    for b in range(REACH + 1):
        start = pl.multiple_of((seq + 32 - REACH + b) % 32 * BLOCK, BLOCK)
        doc_in.append(pltpu.make_async_copy(doc_hbm.at[pl.ds(start, BLOCK)], docs.at[b, 0], doc_sem.at[b]))
        doc_in[-1].start()
    own_q = pltpu.make_async_copy(
        q_hbm.at[:, pl.ds(pl.multiple_of(HEADS * head, HEADS), HEADS), :],
        qb.at[pl.ds(pl.multiple_of(PIECE * head, PIECE), PIECE)], loc_sem.at[1])
    own_q.start()

    barrier = pltpu.get_barrier_semaphore()
    for dx, dc in PEERS:
        pl.semaphore_signal(barrier, inc=1, device_id={"head": to(dx, dc)}, device_id_type=MESH)
    up = (seq // 4) * 4 + (y + 1) % 4
    down = (seq // 4) * 4 + (y + 3) % 4
    for other in (up, down, (seq + 28) % 32):
        pl.semaphore_signal(barrier, inc=1, device_id={"seq": other}, device_id_type=MESH)

    k_in.wait()
    v_in.wait()
    kvs[:, :, 0:128] = jnp.transpose(kin[...], (1, 0, 2))
    kvs[:, :, 128:256] = jnp.transpose(vin[...], (1, 0, 2))
    pl.semaphore_wait(barrier, len(PEERS) + 3)

    def kv_copy(dx, dc, sender):
        target = to(dx, dc)
        rows = pl.ds(pl.multiple_of(REACH * BLOCK + PIECE * sender, PIECE), PIECE)
        return pltpu.make_async_remote_copy(
            kvs.at[target], kv.at[rows, 128:384],
            kv_send.at[2 * dx + dc], kv_recv.at[2 * dx + dc],
            device_id={"head": target}, device_id_type=MESH)

    def q_copy(dx, dc, sender):
        target = to(dx, dc)
        return pltpu.make_async_remote_copy(
            q_hbm.at[:, pl.ds(pl.multiple_of(HEADS * target, HEADS), HEADS), :],
            qb.at[pl.ds(pl.multiple_of(PIECE * sender, PIECE), PIECE)],
            q_send.at[2 * dx + dc], q_recv.at[2 * dx + dc],
            device_id={"head": target}, device_id_type=MESH)

    own_rows = pl.ds(pl.multiple_of(REACH * BLOCK + PIECE * head, PIECE), PIECE)
    own_kv = pltpu.make_async_copy(kvs.at[head], kv.at[own_rows, 128:384], loc_sem.at[0])
    own_kv.start()
    for dx, dc in PEERS:
        kv_copy(dx, dc, head).start()
    for dx, dc in PEERS:
        q_copy(dx, dc, head).start()

    def part(d, dx):
        slot = REACH if d == 0 else d - 1
        return pl.ds(pl.multiple_of(slot * BLOCK + CHUNK * ((x - dx + 4) % 4), CHUNK), CHUNK)

    def pass_on(src, d, dx, target, lane):
        return pltpu.make_async_remote_copy(
            kv.at[part(src, dx), 128:384], kv.at[part(d, dx), 128:384],
            seq_send.at[4 * lane + dx], seq_recv.at[4 * (d - 1) + dx],
            device_id={"seq": target}, device_id_type=MESH)

    def far_send(dx):
        return pass_on(0, 4, dx, (seq + 4) % 32, 0)

    def arrive(d, dx):
        pass_on(d, d, dx, up, 0).wait_recv()

    def own_part(dx):
        if dx == 0:
            own_kv.wait()
        else:
            kv_copy(dx, 0, came(dx, 0)).wait_recv()
        kv_copy(dx, 1, came(dx, 1)).wait_recv()

        @pl.when(seq < 28)
        def _():
            far_send(dx).start()

        @pl.when(y < 3)
        def _():
            pass_on(0, 1, dx, up, 1).start()

        @pl.when(y == 0)
        def _():
            pass_on(0, 3, dx, down, 2).start()

    def far_part(dx):
        @pl.when(behind)
        def _():
            arrive(4, dx)

        @pl.when(behind & (y > 0))
        def _():
            pass_on(4, 3, dx, down, 2).start()

        @pl.when(behind & (y == 3))
        def _():
            pass_on(4, 1, dx, up, 1).start()

    def near_part(dx):
        @pl.when(behind | (y > 0))
        def _():
            arrive(1, dx)

        @pl.when(middle)
        def _():
            pass_on(1, 2, dx, up, 3).start()

    def third_part(dx):
        @pl.when(behind | (y == 3))
        def _():
            arrive(3, dx)

        @pl.when(behind & middle)
        def _():
            pass_on(3, 2, dx, down, 4).start()

    def second_part(dx):
        @pl.when(behind | (y >= 2))
        def _():
            arrive(2, dx)

    nothing = jnp.zeros((BLOCK, 256), jnp.bfloat16)
    for d in range(1, REACH + 1):
        @pl.when((seq < d))
        def _():
            kv[(d - 1) * BLOCK:d * BLOCK, 128:384] = nothing

    lane = lax.broadcasted_iota(jnp.int32, (BLOCK, 128), 1)
    for d in range(REACH + 1):
        doc_in[REACH - d].wait()
        cols = jnp.broadcast_to(docs[REACH - d], (128, BLOCK)).astype(jnp.float32).T.astype(jnp.int32)
        same = cols == lane
        rows = pl.ds((REACH if d == 0 else d - 1) * BLOCK, BLOCK)
        kv[rows, 0:128] = jnp.where(same, 1.0, 0.0).astype(jnp.bfloat16)
        kv[rows, 384:512] = jnp.ones((BLOCK, 128), jnp.bfloat16)
        if d == 0:
            tab[...] = jnp.where(same | (lane >= DOCS), 0.0, -PENALTY)

    def spread(i, _):
        rows = pl.ds(pl.multiple_of(16 * i, 16), 16)
        ab[rows] = jnp.broadcast_to(tab[rows, :][:, None, :], (16, HEADS, 128)).astype(jnp.bfloat16)
        return 0

    lax.fori_loop(0, BLOCK // 16, spread, 0)

    own_part(PARTS[0])
    own_part(PARTS[1])
    own_part(PARTS[2])
    own_part(PARTS[3])
    far_part(PARTS[0])
    near_part(PARTS[0])
    far_part(PARTS[1])
    near_part(PARTS[1])
    far_part(PARTS[2])
    near_part(PARTS[2])
    far_part(PARTS[3])
    near_part(PARTS[3])
    own_q.wait()

    def piece(t):
        o = t // 2
        dx = jnp.where(o < 2, 0, jnp.where(o >= 6, 2, jnp.where(o % 2 == 0, 1, 3)))
        dc = jnp.where((o == 1) | (o == 4) | (o == 5) | (o == 7), 1, 0)
        return dx, dc, 2 * ((x - dx + 4) % 4) + (core + dc) % 2

    def queries_in(t):
        dx, dc, source = piece(t)
        pltpu.make_async_remote_copy(
            q_hbm.at[:, 0:HEADS, :],
            qb.at[pl.ds(pl.multiple_of(PIECE * source, PIECE), PIECE)],
            q_send.at[0], q_recv.at[2 * dx + dc],
            device_id={"head": source}, device_id_type=MESH).wait_recv()

    def token_rows(t):
        _, _, source = piece(t)
        return pl.ds(pl.multiple_of(PIECE * source + TILE * (t % 2), TILE), TILE)

    def window(t):
        _, _, source = piece(t)
        return pl.ds(pl.multiple_of((REACH - 1) * BLOCK + CHUNK * (source // 2), CHUNK), BLOCK + CHUNK)

    near, far = BLOCK, (REACH - 1) * BLOCK
    total = far + BLOCK + CHUNK

    def scores(kind, t, slot):
        rows = token_rows(t)
        left = jnp.concatenate(
            [ab[rows].reshape(ROWS, WIDTH), qb[rows].reshape(ROWS, WIDTH)], axis=1)

        def dots(keys):
            return lax.dot_general(
                left, keys, (((1,), (1,)), ((), ())), preferred_element_type=jnp.float32)

        lo, hi = {"near": (0, near), "far": (near, far), "all": (0, far)}[kind]
        sb[slot, :, lo:hi] = dots(kv[lo:hi, 0:256])
        if kind != "far":
            sb[slot, :, far:total] = dots(kv[window(t), 0:256])

    def weigh(kind, t, slot):
        lo, hi = {"near": (0, near), "far": (near, far), "all": (0, far)}[kind]
        _, _, source = piece(t)
        if kind == "far":
            s = sb[slot, :, lo:hi]
        else:
            first = PIECE * (source % 2) + TILE * (t % 2)
            token = lax.broadcasted_iota(jnp.int32, (ROWS, CHUNK), 0) // HEADS + first
            key = lax.broadcasted_iota(jnp.int32, (ROWS, CHUNK), 1)
            last = jnp.where(key <= token, sb[slot, :, total - CHUNK:total], -PENALTY)
            s = jnp.concatenate([sb[slot, :, lo:hi], sb[slot, :, far:total - CHUNK], last], axis=1)
        top = jnp.max(s, axis=1, keepdims=True)
        if kind == "far":
            old = tops[t, :, 0:1]
            top = jnp.maximum(top, old)
        weights = jnp.exp2((s - top) * SCALE).astype(jnp.bfloat16)
        o = jnp.dot(weights[:, :hi - lo], kv[lo:hi, 256:512], preferred_element_type=jnp.float32)
        if kind != "far":
            o += jnp.dot(weights[:, hi - lo:], kv[window(t), 256:512], preferred_element_type=jnp.float32)
        if kind == "far":
            o += acc[t] * jnp.exp2((old - top) * SCALE)
        if kind == "near":
            acc[t] = o
            tops[t] = jnp.broadcast_to(top, (ROWS, 128))
        else:
            ob[token_rows(t)] = (o[:, :128] / o[:, 128:]).astype(jnp.bfloat16).reshape(TILE, HEADS, WIDTH)

    def run(kind, begin, end, between, after):
        def pair(j, _):
            t = begin + 2 * j
            scores(kind, t + 1, 1)
            weigh(kind, t, 0)
            between(j)
            scores(kind, t + 2, 0)
            weigh(kind, t + 1, 1)
            return 0

        lax.fori_loop(0, (end - begin) // 2 - 1, pair, 0)
        scores(kind, end - 1, 1)
        weigh(kind, end - 2, 0)
        after()
        weigh(kind, end - 1, 1)

    def near_between(j):
        @pl.when(j < 2)
        def _():
            third_part(jnp.where(j == 0, 0, 3))
            third_part(j + 1)

        queries_in(2 * j + 2)

    def near_after():
        for dx in PARTS:
            second_part(dx)
        scores("far", 0, 0)

    def far_after():
        queries_in(EARLY)
        scores("all", EARLY, 0)

    scores("near", 0, 0)
    run("near", 0, EARLY, near_between, near_after)
    run("far", 0, EARLY, lambda j: None, far_after)
    run("all", EARLY, BLOCK // TILE, lambda j: queries_in(EARLY + 2 * j + 2), lambda: None)

    for dx, dc in PEERS:
        kv_copy(dx, dc, head).wait_send()
        q_copy(dx, dc, head).wait_send()
    for dx in PARTS:
        @pl.when(seq < 28)
        def _():
            far_send(dx).wait_send()

        @pl.when(behind | (y < 3))
        def _():
            pass_on(0, 1, dx, up, 1).wait_send()

        @pl.when(behind | (y == 0))
        def _():
            pass_on(0, 3, dx, down, 2).wait_send()

        @pl.when(middle)
        def _():
            pass_on(1, 2, dx, up, 3).wait_send()

        @pl.when(behind & middle)
        def _():
            pass_on(3, 2, dx, down, 4).wait_send()


def per_device(queries, keys, values, doc_ids):
    hbm = pl.BlockSpec(memory_space=pltpu.HBM)
    dma = pltpu.SemaphoreType.DMA
    return pl.pallas_call(
        kernel,
        out_shape=jax.ShapeDtypeStruct((BLOCK, HEADS, WIDTH), jnp.bfloat16),
        in_specs=[hbm] * 4,
        out_specs=pl.BlockSpec(memory_space=pltpu.VMEM),
        scratch_shapes=[
            pltpu.VMEM((PIECE, 8, WIDTH), jnp.bfloat16),
            pltpu.VMEM((PIECE, 8, WIDTH), jnp.bfloat16),
            pltpu.VMEM((8, PIECE, 2 * WIDTH), jnp.bfloat16),
            pltpu.VMEM((8, 1, BLOCK), jnp.int32),
            pltpu.VMEM(((REACH + 1) * BLOCK, 512), jnp.bfloat16),
            pltpu.VMEM((BLOCK, HEADS, WIDTH), jnp.bfloat16),
            pltpu.VMEM((BLOCK, HEADS, WIDTH), jnp.bfloat16),
            pltpu.VMEM((BLOCK, 128), jnp.float32),
            pltpu.VMEM((2, ROWS, WINDOW), jnp.float32),
            pltpu.VMEM((EARLY, ROWS, 2 * WIDTH), jnp.float32),
            pltpu.VMEM((EARLY, ROWS, 128), jnp.float32),
            dma((8,)), dma((8,)), dma((8,)), dma((8,)), dma((20,)), dma((16,)), dma((4,)), dma((5,)),
        ],
        compiler_params=pltpu.CompilerParams(
            collective_id=0, has_side_effects=True, vmem_limit_bytes=40 << 20),
    )(*(pltpu.with_memory_space_constraint(v, pltpu.HBM) for v in (queries, keys, values, doc_ids)))


def solution(mesh):
    spec = P(("seq", "head"), None, None)
    return jax.shard_map(
        per_device, mesh=mesh, in_specs=(spec, spec, spec, P()),
        out_specs=P("seq", "head", None), check_vma=False)
```

time: 58.3 us -> 51.2 us (0.88)
  the two profiles are of different devices: /device:TPU:1 before, /device:TPU:129 now
where the time goes in v3:
time: 51.2 us
  Pallas kernels  49.8 us (97%)
  local copies, waits for them, and re-layouts  1.32 us (3%)
    pallas_call x1, Pallas kernels, per_device(): pl.pallas_call(kernel, out_shape=jax.ShapeDtypeStruct((BLOCK, HEADS, WIDT...  49.8 us
    unnamed x1, local copies, waits for them, and re-layouts  1.32 us

profile of v3, /device:TPU:129, one launch (start us, length us, event | category | flops | bytes accessed | tf_op | source)
XLA Modules:
  0.0 51.2 jit_solution(3705343943958925694)
XLA Ops:
  0.0 49.8 %shard_map.46 = bf16[512,16,128]{2,1,0:T(8,128)(2,1)S(1)} custom-call(bf16[64,128,128]{2,1,0:T(8,128)(2,1)} %q_hbm.1, bf16[64,8,128]{2,1,0:T(8,128)(2,1)} %k_hbm.1, bf16[64,8,128]{2,1,0:T(8,128)(2,1)} %v_hbm.1, s32[16384]{0:T(1024)} %doc_hbm.1), custom_call_target="tpu_custom_call" | custom-call | tf_op jit(solution)/shard_map/pallas_call | solution.py:337
  49.8 1.3 %copy.6 = bf16[512,16,128]{2,1,0:T(8,128)(2,1)} copy(bf16[512,16,128]{2,1,0:T(8,128)(2,1)S(1)} %shard_map.46) | data formatting | bytes 4194304

commit v4 on v3

--- a/solution.py
+++ b/solution.py
@@ -90,8 +90,7 @@
     own_kv.start()
     for dx, dc in PEERS:
         kv_copy(dx, dc, head).start()
-    for dx, dc in PEERS:
-        q_copy(dx, dc, head).start()
+    q_copy(0, 1, head).start()
 
     def part(d, dx):
         slot = REACH if d == 0 else d - 1
@@ -192,6 +191,8 @@
     own_part(PARTS[1])
     own_part(PARTS[2])
     own_part(PARTS[3])
+    for dx, dc in PEERS[1:]:
+        q_copy(dx, dc, head).start()
     far_part(PARTS[0])
     near_part(PARTS[0])
     far_part(PARTS[1])

time: 51.2 us -> 50.3 us (0.982)
  Pallas kernels: 49.8 us -> 48.7 us
    pallas_call x1, Pallas kernels: 49.8 us -> 48.7 us  [per_device(): pl.pallas_call(kernel, out_shape=jax.ShapeDtypeStruct((BLOCK, HEADS, WIDT...]
where the time goes in v4:
time: 50.3 us; the launch traced here: 50 us
  Pallas kernels  48.7 us (97%)
  local copies, waits for them, and re-layouts  1.32 us (3%)
    pallas_call x1, Pallas kernels, per_device(): pl.pallas_call(kernel, out_shape=jax.ShapeDtypeStruct((BLOCK, HEADS, WIDT...  48.7 us
    unnamed x1, local copies, waits for them, and re-layouts  1.32 us

profile of v4, /device:TPU:129, one launch (start us, length us, event | category | flops | bytes accessed | tf_op | source)
XLA Modules:
  0.0 50.0 jit_solution(5011902665761372536)
XLA Ops:
  0.0 48.7 %shard_map.46 = bf16[512,16,128]{2,1,0:T(8,128)(2,1)S(1)} custom-call(bf16[64,128,128]{2,1,0:T(8,128)(2,1)} %q_hbm.1, bf16[64,8,128]{2,1,0:T(8,128)(2,1)} %k_hbm.1, bf16[64,8,128]{2,1,0:T(8,128)(2,1)} %v_hbm.1, s32[16384]{0:T(1024)} %doc_hbm.1), custom_call_target="tpu_custom_call" | custom-call | tf_op jit(solution)/shard_map/pallas_call | solution.py:338
  48.7 1.3 %copy.6 = bf16[512,16,128]{2,1,0:T(8,128)(2,1)} copy(bf16[512,16,128]{2,1,0:T(8,128)(2,1)S(1)} %shard_map.46) | data formatting | bytes 4194304
